TPU v7x, 32 devices: a whole 2x2x4 slice. The times are simulated.
32 devices in a mesh: blk: 8 (over z, y), pix: 4 (over x, core).
Axes of the slice: x: 2, y: 2, z: 4, core: 2. Of those that a mesh axis runs over, the one named last changes fastest.
Arguments:
- images: bfloat16 [256, 16384], P('blk', 'pix'), may hold values from -14 to 14
- templates: bfloat16 [2304, 16384], P('blk', 'pix'), may hold values from -4 to 4
- routes: int32 [256, 4], P('blk'), may hold values from 0 to 7, all different within a row; in each aligned block of 32 rows (0 to 31, 32 to 63, ...) at most 24 rows name the same one
- image_weight: float32 [256], P('blk'), may hold values from 0.25 to 4
- template_weight: float32 [2304], P('blk'), may hold values from 0.25 to 4
Outputs:
- template_means: bfloat16 [2304, 16384], P('blk', 'pix')
- image_duals: float32 [256], P('blk')
Inputs may be any that keep to these rules, and one draw needn't show every extreme that they name: `routes`: each image names 4 different template blocks. Among the 32 images of one block, at most 24 name any one template block, and some template block is named by exactly 24 of them. Every template block is named by some image.
All inputs are finite; a program needn't handle non-finite values.
Results may differ from a plain program's by a relative error of at most 0.0046.
Values may be sent and summed in bfloat16 or wider, within the bound.
A program may use at most 64 MiB of HBM per device.

v0:
```python
import jax
import jax.numpy as jnp
from jax import lax
from jax.sharding import PartitionSpec as P

SWEEPS = 2


def on_device(images, templates, routes, image_weight, template_weight):
    blocks = lax.axis_size("blk")
    img_dev = images.shape[0]
    admits = routes.shape[1]
    capacity = max(2, (3 * img_dev * admits + 2 * blocks - 1) // (2 * blocks))
    target = routes.reshape(-1)
    target_hot = (target[:, None] == jnp.arange(blocks, dtype=jnp.int32)[None, :]).astype(jnp.int32)
    before = jnp.cumsum(target_hot, axis=0) - target_hot
    position = jnp.sum(before * target_hot, axis=1)
    slot_of = target * capacity + position
    wanted = jnp.arange(blocks * capacity, dtype=jnp.int32)
    matches = slot_of[None, :] == wanted[:, None]
    filled = jnp.any(matches, axis=1)
    owner_image = jnp.sum(
        jnp.where(matches, jnp.arange(target.shape[0], dtype=jnp.int32)[None, :] // admits, 0),
        axis=1,
    )
    outgoing = jnp.where(filled[:, None], images[owner_image], jnp.zeros((), images.dtype))
    outgoing = outgoing.reshape(blocks, capacity, images.shape[1])
    slot_flags = filled.astype(jnp.bfloat16).reshape(blocks, capacity)
    template_log = jnp.log(template_weight)
    arrived_piece = lax.all_to_all(outgoing, "blk", split_axis=0, concat_axis=0, tiled=True)
    marks_piece = lax.all_to_all(slot_flags, "blk", split_axis=0, concat_axis=0, tiled=True)
    partial_value = jnp.einsum(
        "bmp,tp->bmt", arrived_piece, templates, preferred_element_type=jnp.float32
    )
    summed = lax.psum(partial_value, "pix")
    usable = marks_piece > 0
    image_log = jnp.log(image_weight)
    slot_duals = jnp.zeros((blocks, capacity), jnp.float32)
    image_duals = jnp.zeros((img_dev,), jnp.float32)
    for sweep_index in range(SWEEPS):
        column_terms = jnp.where(usable[:, :, None], summed + slot_duals[:, :, None], -jnp.inf)
        column_peak = jnp.max(column_terms, axis=(0, 1))
        template_duals = (
            template_log
            - column_peak
            - jnp.log(jnp.sum(jnp.exp(column_terms - column_peak), axis=(0, 1)))
        )
        row_terms = summed + template_duals
        row_peak = jnp.max(row_terms, axis=2)
        row_total = jnp.sum(jnp.exp(row_terms - row_peak[:, :, None]), axis=2)
        levels = row_peak + jnp.log(row_total)
        back_levels = lax.all_to_all(levels, "blk", split_axis=0, concat_axis=0, tiled=True)
        level_routes = back_levels.reshape(-1)[slot_of].reshape(img_dev, admits)
        route_peak = jnp.max(level_routes, axis=1)
        image_duals = (
            image_log
            - route_peak
            - jnp.log(jnp.sum(jnp.exp(level_routes - route_peak[:, None]), axis=1))
        )
        duals_send = jnp.where(filled, image_duals[owner_image], 0.0).reshape(blocks, capacity)
        slot_duals = lax.all_to_all(duals_send, "blk", split_axis=0, concat_axis=0, tiled=True)
    column_terms = jnp.where(usable[:, :, None], summed + slot_duals[:, :, None], -jnp.inf)
    column_peak = jnp.max(column_terms, axis=(0, 1))
    column_exp = jnp.exp(column_terms - column_peak)
    plan_weights = (column_exp / jnp.sum(column_exp, axis=(0, 1))).astype(jnp.bfloat16)
    template_means = jnp.einsum(
        "bmt,bmp->tp", plan_weights, arrived_piece, preferred_element_type=jnp.float32
    ).astype(jnp.bfloat16)
    return (template_means, image_duals)


def solution(mesh):
    in_specs = (P("blk", "pix"), P("blk", "pix"), P("blk", None), P("blk"), P("blk"))
    out_specs = (P("blk", "pix"), P("blk"))
    return jax.shard_map(
        on_device, mesh=mesh, in_specs=in_specs, out_specs=out_specs, check_vma=False
    )
```

profile of v0, /device:TPU:0, one launch (start us, length us, event | category | flops | bytes accessed | tf_op | source)
XLA Modules:
  0.0 203.8 jit_solution(13468316568536961378)
XLA Ops:
  7.2 0.9 copy.17
  9.0 2.7 %gather_fusion = bf16[192,4096]{1,0:T(8,128)(2,1)} fusion(bf16[32,4096]{1,0:T(8,128)(2,1)S(1)} %copy-done.1, s32[1024]{0:T(1024)S(1)} %pad_clamp_fusion.1), kind=kCustom, calls=%fused_computation | custom fusion | bytes 3146496 | tf_op jit(solution)/shard_map/gather | solution.py:26
  11.7 2.7 %broadcast_select_fusion = bf16[8,24,4096]{2,1,0:T(8,128)(2,1)} fusion(bf16[8,24,4096]{2,1,0:T(8,128)(2,1)} %bitcast.88, pred[8,24]{1,0:T(8,128)(4,1)S(1)} %broadcast_in_dim.77), kind=kLoop, calls=%fused_computation.7 | loop fusion | flops 786432 | bytes 3145920 | tf_op jit(solution)/shard_map/jit(_where)/select_n | solution.py:26
  14.4 7.4 %all-to-all-start.1 = ((bf16[8,24,4096]{2,1,0:T(8,128)(2,1)}), bf16[8,24,4096]{2,1,0:T(8,128)(2,1)}, u32[]{:S(2)}, u32[]{:S(2)}) async-start(bf16[8,24,4096]{2,1,0:T(8,128)(2,1)} %broadcast_select_fusion), calls=%async_computation.1 | async-start | bytes 3145728 | tf_op jit(solution)/shard_map/all_to_all | solution.py:30
  22.8 36.2 %all-to-all-done.1 = bf16[8,24,4096]{2,1,0:T(8,128)(2,1)} async-done(((bf16[8,24,4096]{2,1,0:T(8,128)(2,1)}), bf16[8,24,4096]{2,1,0:T(8,128)(2,1)}, u32[]{:S(2)}, u32[]{:S(2)}) %all-to-all-start.1) | async-done | bytes 1572896 | tf_op jit(solution)/shard_map/all_to_all | solution.py:30
  59.0 3.6 %all-to-all-start = ((bf16[8,1,24]{2,1,0:T(2,128)(2,1)}), bf16[8,1,24]{2,1,0:T(2,128)(2,1)S(1)}, u32[]{:S(2)}, u32[]{:S(2)}) async-start(bf16[8,1,24]{2,1,0:T(2,128)(2,1)} %reshape.347), calls=%async_computation | async-start | bytes 8192 | tf_op jit(solution)/shard_map/all_to_all | solution.py:31
  62.7 3.3 %fusion.1 = f32[8,24,288]{2,1,0:T(8,128)} fusion(bf16[8,24,4096]{2,1,0:T(8,128)(2,1)} %all-to-all-done.1, bf16[288,4096]{1,0:T(8,128)(2,1)S(1)} %copy-done), kind=kOutput, calls=%fused_computation.5 | convolution fusion | flops 452984832 | bytes 4153344 | tf_op jit(solution)/shard_map/bmp,tp->bmt/dot_general | solution.py:32
  66.0 3.1 %all-to-all-done = bf16[8,1,24]{2,1,0:T(2,128)(2,1)S(1)} async-done(((bf16[8,1,24]{2,1,0:T(2,128)(2,1)}), bf16[8,1,24]{2,1,0:T(2,128)(2,1)S(1)}, u32[]{:S(2)}, u32[]{:S(2)}) %all-to-all-start) | async-done | bytes 416 | tf_op jit(solution)/shard_map/all_to_all | solution.py:31
  69.1 31.1 %all-reduce.2.cloned.1.call-done = f32[8,24,288]{2,1,0:T(8,128)} async-done(((f32[8,24,288]{2,1,0:T(8,128)}), f32[8,24,288]{2,1,0:T(8,128)}) %all-reduce.2.cloned.1.call-update) | async-done | bytes 221200 | tf_op jit(solution)/shard_map/psum | solution.py:35
  100.2 1.1 select_reduce_fusion
  101.3 1.1 exponential_reduce_fusion.3
  102.5 1.1 add_reduce_fusion.1
  103.5 1.2 exponential_reduce_fusion.2
  105.3 5.5 %all-to-all-start.2 = ((f32[8,1,24]{2,1,0:T(1,128)}), f32[8,1,24]{2,1,0:T(1,128)S(1)}, u32[]{:S(2)}, u32[]{:S(2)}) async-start(f32[8,1,24]{2,1,0:T(1,128)} %bitcast.5), calls=%async_computation.2 | async-start | bytes 8192 | tf_op jit(solution)/shard_map/all_to_all | solution.py:52
  110.8 6.4 %all-to-all-done.2 = f32[8,1,24]{2,1,0:T(1,128)S(1)} async-done(((f32[8,1,24]{2,1,0:T(1,128)}), f32[8,1,24]{2,1,0:T(1,128)S(1)}, u32[]{:S(2)}, u32[]{:S(2)}) %all-to-all-start.2) | async-done | bytes 800 | tf_op jit(solution)/shard_map/all_to_all | solution.py:52
  118.5 1.3 gather_fusion.1
  121.6 19.9 %select_select_fusion.1 = f32[192]{0:T(256)S(1)} fusion(pred[192]{0:T(512)(128)(4,1)S(1)} %fusion.11, f32[]{:T(128)} %bitcast.8, f32[]{:T(128)} %bitcast.9, f32[]{:T(128)} %bitcast.10, f32[]{:T(128)} %bitcast.11, f32[]{:T(128)} %bitcast.12, f32[]{:T(128)} %bitcast.13, f32[]{:T(128)} %bitcast.14, f32[]{:T(128)} %bitcast.15, f32[]{:T(128)} %bitcast.16, ...), kind=kLoop, calls=%fused_computation.46 | loop fusion | flops 12096 | bytes 1856 | tf_op jit(solution)/shard_map/jit(_where)/select_n | solution.py:60
  141.6 8.8 %all_to_all.35 = f32[8,1,24]{2,1,0:T(1,128)S(1)} all-to-all(f32[8,1,24]{2,1,0:T(1,128)S(1)} %select_n.88), channel_id=1, replica_groups=mesh['blk'=8,'pix'=4] {'blk'}, dimensions={0} | all-to-all | bytes 1536 | tf_op jit(solution)/shard_map/all_to_all | solution.py:61
  151.1 8.9 %all_to_all.36 = f32[8,1,24]{2,1,0:T(1,128)S(1)} all-to-all(f32[8,1,24]{2,1,0:T(1,128)S(1)} %bitcast.97), channel_id=1, replica_groups=mesh['blk'=8,'pix'=4] {'blk'}, dimensions={0} | all-to-all | bytes 1536 | tf_op jit(solution)/shard_map/all_to_all | solution.py:52
  160.7 1.3 gather_fusion.2
  163.1 0.7 fusion.15
  163.8 20.1 %select_select_fusion = f32[192]{0:T(256)S(1)} fusion(pred[192]{0:T(512)(128)(4,1)S(1)} %fusion.11, f32[]{:T(128)} %bitcast.42, f32[]{:T(128)} %bitcast.43, f32[]{:T(128)} %bitcast.44, f32[]{:T(128)} %bitcast.45, f32[]{:T(128)} %bitcast.46, f32[]{:T(128)} %bitcast.47, f32[]{:T(128)} %bitcast.48, f32[]{:T(128)} %bitcast.49, f32[]{:T(128)} %bitcast.50, ...), kind=kLoop, calls=%fused_computation.45 | loop fusion | flops 12096 | bytes 1856 | tf_op jit(solution)/shard_map/jit(_where)/select_n | solution.py:60
  184.0 8.8 %all_to_all.37 = f32[8,1,24]{2,1,0:T(1,128)S(1)} all-to-all(f32[8,1,24]{2,1,0:T(1,128)S(1)} %select_n.91), channel_id=1, replica_groups=mesh['blk'=8,'pix'=4] {'blk'}, dimensions={0} | all-to-all | bytes 1536 | tf_op jit(solution)/shard_map/all_to_all | solution.py:61
  193.2 3.7 %fusion = bf16[288,4096]{1,0:T(8,128)(2,1)} fusion(bf16[8,24,4096]{2,1,0:T(8,128)(2,1)} %all-to-all-done.1, f32[8,24,288]{2,1,0:T(8,128)S(1)} %copy-done.2, f32[288]{0:T(512)S(1)} %fusion.5, f32[288]{0:T(512)S(1)} %fusion.4, f32[8,24]{1,0:T(8,128)S(1)} %bitcast.91, pred[8,24]{1,0:T(8,128)(4,1)S(1)} %compare_bitcast_fusion), kind=kOutput, calls=%fused_computation.4 | convolution fusion | flops 454440960 | bytes 4156608 | tf_op jit(solution)/shard_map/bmt,bmp->tp/dot_general | solution.py:66
  (62 shorter events, 8.5 us)
Async XLA Ops:
  7.2 55.5 %copy-start = (bf16[288,4096]{1,0:T(8,128)(2,1)S(1)}, bf16[288,4096]{1,0:T(8,128)(2,1)}, u32[]{:S(2)}) copy-start(bf16[288,4096]{1,0:T(8,128)(2,1)} %param.6) | copy-start | bytes 7077892
  7.2 1.8 copy-start.1
  14.4 7.5 %copy-start.4 = (s32[32,4]{0,1:T(4,128)S(1)}, s32[32,4]{0,1:T(4,128)}, u32[]{:S(2)}) copy-start(s32[32,4]{0,1:T(4,128)} %param.7) | copy-start | bytes 1540
  14.4 44.5 %all-to-all-start.1 = ((bf16[8,24,4096]{2,1,0:T(8,128)(2,1)}), bf16[8,24,4096]{2,1,0:T(8,128)(2,1)}, u32[]{:S(2)}, u32[]{:S(2)}) async-start(bf16[8,24,4096]{2,1,0:T(8,128)(2,1)} %broadcast_select_fusion), calls=%async_computation.1 | async-start | bytes 3145728 | tf_op jit(solution)/shard_map/all_to_all | solution.py:30
  59.0 10.1 %all-to-all-start = ((bf16[8,1,24]{2,1,0:T(2,128)(2,1)}), bf16[8,1,24]{2,1,0:T(2,128)(2,1)S(1)}, u32[]{:S(2)}, u32[]{:S(2)}) async-start(bf16[8,1,24]{2,1,0:T(2,128)(2,1)} %reshape.347), calls=%async_computation | async-start | bytes 8192 | tf_op jit(solution)/shard_map/all_to_all | solution.py:31
  62.6 39.8 %copy-start.5 = (f32[288]{0:T(512)S(1)}, f32[288]{0:T(512)}, u32[]{:S(2)}) copy-start(f32[288]{0:T(512)} %param.9) | copy-start | bytes 3460
  62.6 37.6 %all-reduce.2.cloned.1.call-start = ((), (), s32[]{:S(2)}) async-start(), calls=%async_computation.6 | async-start | bytes 589824 | tf_op jit(solution)/shard_map/psum | solution.py:35
  66.0 54.2 %copy-start.6 = (f32[32]{0:T(128)S(1)}, f32[32]{0:T(128)}, u32[]{:S(2)}) copy-start(f32[32]{0:T(128)} %param.8) | copy-start | bytes 388
  100.2 50.3 %copy-start.2 = (f32[8,24,288]{2,1,0:T(8,128)S(1)}, f32[8,24,288]{2,1,0:T(8,128)}, u32[]{:S(2)}) copy-start(f32[8,24,288]{2,1,0:T(8,128)} %all-reduce.2.cloned.1.call-done) | copy-start | bytes 663556
  105.3 11.9 %all-to-all-start.2 = ((f32[8,1,24]{2,1,0:T(1,128)}), f32[8,1,24]{2,1,0:T(1,128)S(1)}, u32[]{:S(2)}, u32[]{:S(2)}) async-start(f32[8,1,24]{2,1,0:T(1,128)} %bitcast.5), calls=%async_computation.2 | async-start | bytes 8192 | tf_op jit(solution)/shard_map/all_to_all | solution.py:52
  162.4 34.5 %copy-start.3 = (f32[32]{0:T(128)}, f32[32]{0:T(128)S(1)}, u32[]{:S(2)}) copy-start(f32[32]{0:T(128)S(1)} %log_subtract_fusion.2) | copy-start | bytes 388
Sparse Core Ops, SparseCore 0:
  66.3 33.7 all-reduce.1
where the time goes:
time: 205 us; the launch traced here: 204 us
  waiting for transfers between devices  76.8 us (37%)
  other arithmetic  51.3 us (25%)
  blocking collectives  26.6 us (13%)
  starting transfers between devices  16.6 us (8%)
  between operations  14.3 us (7%)
  local copies, waits for them, and re-layouts  11.1 us (5%)
  matrix products  7.05 us (3%)
    select_n x2, other arithmetic, on_device(): jnp.where(filled, image_duals[owner_image], 0.0).reshape(blocks, capacity)  40 us
    all_to_all x1, waiting for transfers between devices, on_device(): lax.all_to_all(outgoing, 'blk', split_axis=0, concat_axis=0, tiled=True)  36.2 us
    psum x1, waiting for transfers between devices, on_device(): summed = lax.psum(partial_value, 'pix')  31.1 us
    all_to_all x2, blocking collectives, on_device(): lax.all_to_all(duals_send, 'blk', split_axis=0, concat_axis=0, tiled=True)  17.7 us
    all_to_all x1, blocking collectives, on_device(): lax.all_to_all(levels, 'blk', split_axis=0, concat_axis=0, tiled=True)  8.86 us
    all_to_all x1, starting transfers between devices, on_device(): lax.all_to_all(outgoing, 'blk', split_axis=0, concat_axis=0, tiled=True)  7.44 us
    all_to_all x1, waiting for transfers between devices, on_device(): lax.all_to_all(levels, 'blk', split_axis=0, concat_axis=0, tiled=True)  6.41 us
    all_to_all x1, starting transfers between devices, on_device(): lax.all_to_all(levels, 'blk', split_axis=0, concat_axis=0, tiled=True)  5.52 us
  transfers between devices with their start and end apart: 4, of which 4 were waited for; matrix products, arithmetic and copies ran while one was open for 2% of the time, Pallas kernels for 0%

commit v1 on v0

--- a/solution.py
+++ b/solution.py
@@ -32,7 +32,7 @@
     partial_value = jnp.einsum(
         "bmp,tp->bmt", arrived_piece, templates, preferred_element_type=jnp.float32
     )
-    summed = lax.psum(partial_value, "pix")
+    summed = jnp.sum(lax.all_gather(partial_value, "pix"), axis=0)
     usable = marks_piece > 0
     image_log = jnp.log(image_weight)
     slot_duals = jnp.zeros((blocks, capacity), jnp.float32)

time: 205 us -> 166 us (0.81)
  waiting for transfers between devices: 76.8 us -> 43.6 us
  between operations: 14.3 us -> 0.94 us
  blocking collectives: 26.6 us -> 37.7 us
  other arithmetic: 51.3 us -> 49 us
    psum x1 -> x0, waiting for transfers between devices: 31.1 us -> none  [on_device(): summed = lax.psum(partial_value, 'pix')]
    all_gather x0 -> x1, blocking collectives: none -> 11.2 us  [on_device(): summed = jnp.sum(lax.all_gather(partial_value, 'pix'), axis=0)]
    all_to_all x1, starting transfers between devices: 3.64 us -> 7.31 us  [on_device(): lax.all_to_all(slot_flags, 'blk', split_axis=0, concat_axis=0, tiled=True)]
    all_to_all x1, waiting for transfers between devices: 3.09 us -> 0.86 us  [on_device(): lax.all_to_all(slot_flags, 'blk', split_axis=0, concat_axis=0, tiled=True)]
    all_to_all x1, starting transfers between devices: 7.44 us -> 5.27 us  [on_device(): lax.all_to_all(outgoing, 'blk', split_axis=0, concat_axis=0, tiled=True)]
  transfers between devices with their start and end apart: 4 -> 3, of which waited for: 4 -> 3; matrix products, arithmetic and copies ran while one was open for 2% -> 4% of each run, Pallas kernels for 0% -> 0%
where the time goes in v1:
time: 166 us; the launch traced here: 165 us
  other arithmetic  49 us (30%)
  waiting for transfers between devices  43.6 us (26%)
  blocking collectives  37.7 us (23%)
  starting transfers between devices  16.2 us (10%)
  local copies, waits for them, and re-layouts  11.1 us (7%)
  matrix products  6.33 us (4%)
    select_n x2, other arithmetic, on_device(): jnp.where(filled, image_duals[owner_image], 0.0).reshape(blocks, capacity)  40.2 us
    all_to_all x1, waiting for transfers between devices, on_device(): lax.all_to_all(outgoing, 'blk', split_axis=0, concat_axis=0, tiled=True)  36.3 us
    all_to_all x2, blocking collectives, on_device(): lax.all_to_all(duals_send, 'blk', split_axis=0, concat_axis=0, tiled=True)  17.7 us
    all_gather x1, blocking collectives, on_device(): summed = jnp.sum(lax.all_gather(partial_value, 'pix'), axis=0)  11.2 us
    all_to_all x1, blocking collectives, on_device(): lax.all_to_all(levels, 'blk', split_axis=0, concat_axis=0, tiled=True)  8.86 us
    all_to_all x1, starting transfers between devices, on_device(): lax.all_to_all(slot_flags, 'blk', split_axis=0, concat_axis=0, tiled=True)  7.31 us
    all_to_all x1, waiting for transfers between devices, on_device(): lax.all_to_all(levels, 'blk', split_axis=0, concat_axis=0, tiled=True)  6.41 us
    all_to_all x1, starting transfers between devices, on_device(): lax.all_to_all(outgoing, 'blk', split_axis=0, concat_axis=0, tiled=True)  5.27 us
  transfers between devices with their start and end apart: 3, of which 3 were waited for; matrix products, arithmetic and copies ran while one was open for 4% of the time, Pallas kernels for 0%

profile of v1, /device:TPU:0, one launch (start us, length us, event | category | flops | bytes accessed | tf_op | source)
XLA Modules:
  0.0 165.0 jit_solution(6401863094919313721)
XLA Ops:
  0.7 0.9 copy.17
  3.0 7.3 %all-to-all-start = ((bf16[8,1,24]{2,1,0:T(2,128)(2,1)}), bf16[8,1,24]{2,1,0:T(2,128)(2,1)S(1)}, u32[]{:S(2)}, u32[]{:S(2)}) async-start(bf16[8,1,24]{2,1,0:T(2,128)(2,1)} %reshape.348), calls=%async_computation | async-start | bytes 8192 | tf_op jit(solution)/shard_map/all_to_all | solution.py:31
  10.5 2.7 %gather_fusion = bf16[192,4096]{1,0:T(8,128)(2,1)} fusion(bf16[32,4096]{1,0:T(8,128)(2,1)S(1)} %copy-done.1, s32[1024]{0:T(1024)S(1)} %pad_clamp_fusion.1), kind=kCustom, calls=%fused_computation | custom fusion | bytes 3146496 | tf_op jit(solution)/shard_map/gather | solution.py:26
  13.2 2.7 %broadcast_select_fusion = bf16[8,24,4096]{2,1,0:T(8,128)(2,1)} fusion(bf16[8,24,4096]{2,1,0:T(8,128)(2,1)} %bitcast.89, pred[8,24]{1,0:T(8,128)(4,1)S(1)} %broadcast_in_dim.77), kind=kLoop, calls=%fused_computation.7 | loop fusion | flops 786432 | bytes 3145920 | tf_op jit(solution)/shard_map/jit(_where)/select_n | solution.py:26
  15.9 0.9 all-to-all-done
  16.8 5.3 %all-to-all-start.1 = ((bf16[8,24,4096]{2,1,0:T(8,128)(2,1)}), bf16[8,24,4096]{2,1,0:T(8,128)(2,1)}, u32[]{:S(2)}, u32[]{:S(2)}) async-start(bf16[8,24,4096]{2,1,0:T(8,128)(2,1)} %broadcast_select_fusion), calls=%async_computation.1 | async-start | bytes 3145728 | tf_op jit(solution)/shard_map/all_to_all | solution.py:30
  22.3 36.3 %all-to-all-done.1 = bf16[8,24,4096]{2,1,0:T(8,128)(2,1)} async-done(((bf16[8,24,4096]{2,1,0:T(8,128)(2,1)}), bf16[8,24,4096]{2,1,0:T(8,128)(2,1)}, u32[]{:S(2)}, u32[]{:S(2)}) %all-to-all-start.1) | async-done | bytes 1572896 | tf_op jit(solution)/shard_map/all_to_all | solution.py:30
  58.6 2.6 %fusion.1 = f32[8,24,288]{2,1,0:T(8,128)S(1)} fusion(bf16[8,24,4096]{2,1,0:T(8,128)(2,1)} %all-to-all-done.1, bf16[288,4096]{1,0:T(8,128)(2,1)S(1)} %copy-done), kind=kOutput, calls=%fused_computation.5 | convolution fusion | flops 452984832 | bytes 4153344 | tf_op jit(solution)/shard_map/bmp,tp->bmt/dot_general | solution.py:32
  61.2 11.2 %all-gather = f32[32,24,288]{2,1,0:T(8,128)} all-gather(f32[8,24,288]{2,1,0:T(8,128)S(1)} %fusion.1), channel_id=2, replica_groups=mesh['blk'=8,'pix'=4] {'pix'}, dimensions={0}, use_global_device_ids=true | all-gather | bytes 1105920 | tf_op jit(solution)/shard_map/all_gather | solution.py:35
  72.4 1.4 reduce_sum.97
  75.0 3.6 %all-to-all-start.2 = ((f32[8,1,24]{2,1,0:T(1,128)}), f32[8,1,24]{2,1,0:T(1,128)S(1)}, u32[]{:S(2)}, u32[]{:S(2)}) async-start(f32[8,1,24]{2,1,0:T(1,128)} %bitcast.6), calls=%async_computation.2 | async-start | bytes 8192 | tf_op jit(solution)/shard_map/all_to_all | solution.py:52
  78.6 6.4 %all-to-all-done.2 = f32[8,1,24]{2,1,0:T(1,128)S(1)} async-done(((f32[8,1,24]{2,1,0:T(1,128)}), f32[8,1,24]{2,1,0:T(1,128)S(1)}, u32[]{:S(2)}, u32[]{:S(2)}) %all-to-all-start.2) | async-done | bytes 800 | tf_op jit(solution)/shard_map/all_to_all | solution.py:52
  86.3 1.3 gather_fusion.1
  88.0 0.7 fusion.18
  88.7 0.7 fusion.17
  89.4 20.1 %select_select_fusion.1 = f32[192]{0:T(256)S(1)} fusion(pred[192]{0:T(512)(128)(4,1)S(1)} %fusion.11, f32[]{:T(128)} %bitcast.9, f32[]{:T(128)} %bitcast.10, f32[]{:T(128)} %bitcast.11, f32[]{:T(128)} %bitcast.12, f32[]{:T(128)} %bitcast.13, f32[]{:T(128)} %bitcast.14, f32[]{:T(128)} %bitcast.15, f32[]{:T(128)} %bitcast.16, f32[]{:T(128)} %bitcast.17, ...), kind=kLoop, calls=%fused_computation.46 | loop fusion | flops 12096 | bytes 1856 | tf_op jit(solution)/shard_map/jit(_where)/select_n | solution.py:60
  109.6 8.8 %all_to_all.35 = f32[8,1,24]{2,1,0:T(1,128)S(1)} all-to-all(f32[8,1,24]{2,1,0:T(1,128)S(1)} %select_n.88), channel_id=1, replica_groups=mesh['blk'=8,'pix'=4] {'blk'}, dimensions={0} | all-to-all | bytes 1536 | tf_op jit(solution)/shard_map/all_to_all | solution.py:61
  119.1 8.9 %all_to_all.36 = f32[8,1,24]{2,1,0:T(1,128)S(1)} all-to-all(f32[8,1,24]{2,1,0:T(1,128)S(1)} %bitcast.99), channel_id=1, replica_groups=mesh['blk'=8,'pix'=4] {'blk'}, dimensions={0} | all-to-all | bytes 1536 | tf_op jit(solution)/shard_map/all_to_all | solution.py:52
  128.7 1.3 gather_fusion.2
  130.4 0.7 fusion.16
  131.2 0.7 fusion.15
  131.9 20.1 %select_select_fusion = f32[192]{0:T(256)S(1)} fusion(pred[192]{0:T(512)(128)(4,1)S(1)} %fusion.11, f32[]{:T(128)} %bitcast.43, f32[]{:T(128)} %bitcast.44, f32[]{:T(128)} %bitcast.45, f32[]{:T(128)} %bitcast.46, f32[]{:T(128)} %bitcast.47, f32[]{:T(128)} %bitcast.48, f32[]{:T(128)} %bitcast.49, f32[]{:T(128)} %bitcast.50, f32[]{:T(128)} %bitcast.51, ...), kind=kLoop, calls=%fused_computation.45 | loop fusion | flops 12096 | bytes 1856 | tf_op jit(solution)/shard_map/jit(_where)/select_n | solution.py:60
  152.1 8.8 %all_to_all.37 = f32[8,1,24]{2,1,0:T(1,128)S(1)} all-to-all(f32[8,1,24]{2,1,0:T(1,128)S(1)} %select_n.91), channel_id=1, replica_groups=mesh['blk'=8,'pix'=4] {'blk'}, dimensions={0} | all-to-all | bytes 1536 | tf_op jit(solution)/shard_map/all_to_all | solution.py:61
  161.2 3.7 %fusion = bf16[288,4096]{1,0:T(8,128)(2,1)} fusion(bf16[8,24,4096]{2,1,0:T(8,128)(2,1)} %all-to-all-done.1, f32[8,24,288]{2,1,0:T(8,128)S(1)} %reduce_sum.97, f32[288]{0:T(512)S(1)} %fusion.5, f32[288]{0:T(512)S(1)} %fusion.4, f32[8,24]{1,0:T(8,128)S(1)} %bitcast.93, pred[8,24]{1,0:T(8,128)(4,1)S(1)} %compare_bitcast_fusion), kind=kOutput, calls=%fused_computation.4 | convolution fusion | flops 454440960 | bytes 4156608 | tf_op jit(solution)/shard_map/bmt,bmp->tp/dot_general | solution.py:66
  (59 shorter events, 6.8 us)
Async XLA Ops:
  0.6 58.0 %copy-start = (bf16[288,4096]{1,0:T(8,128)(2,1)S(1)}, bf16[288,4096]{1,0:T(8,128)(2,1)}, u32[]{:S(2)}) copy-start(bf16[288,4096]{1,0:T(8,128)(2,1)} %param.6) | copy-start | bytes 7077892
  0.6 9.9 %copy-start.1 = (bf16[32,4096]{1,0:T(8,128)(2,1)S(1)}, bf16[32,4096]{1,0:T(8,128)(2,1)}, u32[]{:S(2)}) copy-start(bf16[32,4096]{1,0:T(8,128)(2,1)} %param.5) | copy-start | bytes 786436
  3.0 13.8 %all-to-all-start = ((bf16[8,1,24]{2,1,0:T(2,128)(2,1)}), bf16[8,1,24]{2,1,0:T(2,128)(2,1)S(1)}, u32[]{:S(2)}, u32[]{:S(2)}) async-start(bf16[8,1,24]{2,1,0:T(2,128)(2,1)} %reshape.348), calls=%async_computation | async-start | bytes 8192 | tf_op jit(solution)/shard_map/all_to_all | solution.py:31
  15.9 6.1 %copy-start.3 = (s32[32,4]{0,1:T(4,128)S(1)}, s32[32,4]{0,1:T(4,128)}, u32[]{:S(2)}) copy-start(s32[32,4]{0,1:T(4,128)} %param.7) | copy-start | bytes 1540
  16.8 41.8 %all-to-all-start.1 = ((bf16[8,24,4096]{2,1,0:T(8,128)(2,1)}), bf16[8,24,4096]{2,1,0:T(8,128)(2,1)}, u32[]{:S(2)}, u32[]{:S(2)}) async-start(bf16[8,24,4096]{2,1,0:T(8,128)(2,1)} %broadcast_select_fusion), calls=%async_computation.1 | async-start | bytes 3145728 | tf_op jit(solution)/shard_map/all_to_all | solution.py:30
  61.2 12.8 %copy-start.4 = (f32[288]{0:T(512)S(1)}, f32[288]{0:T(512)}, u32[]{:S(2)}) copy-start(f32[288]{0:T(512)} %param.9) | copy-start | bytes 3460
  72.4 15.6 %copy-start.5 = (f32[32]{0:T(128)S(1)}, f32[32]{0:T(128)}, u32[]{:S(2)}) copy-start(f32[32]{0:T(128)} %param.8) | copy-start | bytes 388
  75.0 10.1 %all-to-all-start.2 = ((f32[8,1,24]{2,1,0:T(1,128)}), f32[8,1,24]{2,1,0:T(1,128)S(1)}, u32[]{:S(2)}, u32[]{:S(2)}) async-start(f32[8,1,24]{2,1,0:T(1,128)} %bitcast.6), calls=%async_computation.2 | async-start | bytes 8192 | tf_op jit(solution)/shard_map/all_to_all | solution.py:52
  130.4 34.5 %copy-start.2 = (f32[32]{0:T(128)}, f32[32]{0:T(128)S(1)}, u32[]{:S(2)}) copy-start(f32[32]{0:T(128)S(1)} %log_subtract_fusion.2) | copy-start | bytes 388
